TPU v7x, 256 devices: a whole 4x4x8 slice. The times are simulated.
256 devices in a mesh: slab: 64 (over y, z, x_lo), ffn: 4 (over x_hi, core).
Axes of the slice: x: 4 (x_hi: 2, x_lo: 2; x = x_hi * 2 + x_lo), y: 4, z: 8, core: 2. Of those that a mesh axis runs over, the one named last changes fastest.
Arguments:
- tokens: bfloat16 [32768, 512], P('slab'), may hold values from -6 to 6
- gain_attn: float32 [512], replicated, may hold values from 0.1 to 1.9
- w_reduce: bfloat16 [4096, 512], replicated, may hold values from -0.09375 to 0.09375
- gain_keys: float32 [512], replicated, may hold values from 0.1 to 1.9
- w_query: bfloat16 [512, 512], P(None, 'ffn'), may hold values from -1.5 to 1.5
- w_key: bfloat16 [512, 512], P(None, 'ffn'), may hold values from -1.5 to 1.5
- w_value: bfloat16 [512, 512], P(None, 'ffn'), may hold values from -0.25 to 0.25
- w_out: bfloat16 [512, 512], P('ffn'), may hold values from -1.796875 to 1.796875
- gain_ffn: float32 [512], replicated, may hold values from 0.1 to 1.9
- w_up: bfloat16 [512, 2048], P(None, 'ffn'), may hold values from -0.25 to 0.25
- w_depth: float32 [27, 2048], P(None, 'ffn'), may hold values from -1.25 to 1.25
- w_down: bfloat16 [2048, 512], P('ffn'), may hold values from -0.125 to 0.125
- grad_out: bfloat16 [32768, 512], P('slab'), may hold values from -0.0625 to 0.0625
Outputs:
- attended: bfloat16 [32768, 512], P('slab')
- grad_up: float32 [512, 2048], P('slab', 'ffn')
- grad_down: float32 [512, 2048], P('slab', 'ffn')
All inputs are finite; a program needn't handle non-finite values.
Results may differ from a plain program's by a relative error of at most 0.024.
The roundings to bfloat16 on the way count: a program that leaves them out, or rounds other values in their place, can miss the bound.
Values may be sent and summed in bfloat16 or wider, within the bound.
A program may use at most 64 MiB of HBM per device.

v0:
```python
import math
import jax
import jax.numpy as jnp
from jax import lax
from jax.sharding import PartitionSpec as P

HEAD = 64
GX = 16
GY = 16
CZ = 2
EPSILON = 1e-05
ROPE_BASE = 100.0
ROOT_HALF = 0.7071067811865476
NORMAL_SCALE = 0.3989422804014327


def padded_2(cells, sides, width):
    for axis, dim in sides:
        count = lax.axis_size(axis)
        ends = count - 1
        head = lax.slice_in_dim(cells, 0, width, axis=dim)
        tail = lax.slice_in_dim(cells, cells.shape[dim] - width, cells.shape[dim], axis=dim)
        cells = jnp.concatenate(
            [
                lax.ppermute(tail, axis, [(i, (i + 1) % count) for i in range(ends)]),
                cells,
                lax.ppermute(head, axis, [((i + 1) % count, i) for i in range(ends)]),
            ],
            axis=dim,
        )
    return cells


def layer_norm(values, scale_gain):
    values = values.astype(jnp.float32)
    centered = values - jnp.mean(values, axis=-1, keepdims=True)
    variance = jnp.mean(centered * centered, axis=-1, keepdims=True)
    return centered * lax.rsqrt(variance + EPSILON) * scale_gain


def rope_tables(coord_x, coord_y, coord_z, head_size):
    pair_count = head_size // 2
    position = jnp.arange(pair_count, dtype=jnp.int32)
    axis_pick = position % 3
    per_axis = (pair_count + 2) // 3
    frequency = ROPE_BASE ** (-(position // 3).astype(jnp.float32) / per_axis)
    angles = (
        coord_x[:, None] * (axis_pick == 0)
        + coord_y[:, None] * (axis_pick == 1)
        + coord_z[:, None] * (axis_pick == 2)
    ) * frequency
    return (jnp.cos(angles)[:, None, :], jnp.sin(angles)[:, None, :])


def token_tables(first_plane, planes, head_size):
    position = jnp.arange(planes * GY * GX, dtype=jnp.int32)
    coord_x = (position % GX).astype(jnp.float32)
    coord_y = (position // GX % GY).astype(jnp.float32)
    coord_z = (first_plane + position // (GX * GY)).astype(jnp.float32)
    return rope_tables(coord_x, coord_y, coord_z, head_size)


def key_tables(first_row, row_count, head_size):
    position = first_row + jnp.arange(row_count, dtype=jnp.int32)
    half_x = GX // 2
    half_y = GY // 2
    coord_x = (position % half_x).astype(jnp.float32) * 2.0 + 0.5
    coord_y = (position // half_x % half_y).astype(jnp.float32) * 2.0 + 0.5
    coord_z = (position // (half_x * half_y)).astype(jnp.float32) * 2.0 + 0.5
    return rope_tables(coord_x, coord_y, coord_z, head_size)


def rotate(values, cosine, sine_table):
    half_size = values.shape[-1] // 2
    front_half = values[..., :half_size]
    back_half = values[..., half_size:]
    return jnp.concatenate(
        [
            front_half * cosine - back_half * sine_table,
            back_half * cosine + front_half * sine_table,
        ],
        axis=-1,
    )


def make_patches(normed, planes):
    width = normed.shape[-1]
    cell_grid = normed.reshape(planes // 2, 2, GY // 2, 2, GX // 2, 2, width)
    return cell_grid.transpose(0, 2, 4, 1, 3, 5, 6).reshape(-1, 8 * width)


def depth_conv(padded, weights, planes):
    height = padded.shape[1] - 2
    width_x = padded.shape[2] - 2
    result = jnp.zeros((planes, height, width_x, padded.shape[3]), jnp.float32)
    for offset in range(27):
        shift_z = offset // 9
        shift_y = offset // 3 % 3
        shift_x = offset % 3
        window = padded[
            shift_z : shift_z + planes, shift_y : shift_y + height, shift_x : shift_x + width_x
        ]
        result = result + window.astype(jnp.float32) * weights[offset]
    return result


def attend_piece(state_tuple, queries, key_rows, value_rows):
    row_max, row_sum, weighted = state_tuple
    score_scale = key_rows.shape[-1] ** (-0.5)
    scores = (
        jnp.einsum("qhd,khd->hqk", queries, key_rows, preferred_element_type=jnp.float32)
        * score_scale
    )
    new_max = jnp.maximum(row_max, jnp.max(scores, axis=2))
    rescale = jnp.exp(row_max - new_max)
    expo = jnp.exp(scores - new_max[:, :, None])
    row_sum = row_sum * rescale + jnp.sum(expo, axis=2)
    weighted = weighted * rescale[:, :, None] + jnp.einsum(
        "hqk,khd->hqd", expo.astype(jnp.bfloat16), value_rows, preferred_element_type=jnp.float32
    )
    return (new_max, row_sum, weighted)


def per_device(
    tokens,
    gain_attn,
    w_reduce,
    gain_keys,
    w_query,
    w_key,
    w_value,
    w_out,
    gain_ffn,
    w_up,
    w_depth,
    w_down,
    grad_out,
):
    slab_index = lax.axis_index("slab")
    tok_rows = tokens.shape[0]
    heads_dev = w_query.shape[1] // HEAD
    normed = layer_norm(tokens, gain_attn).astype(jnp.bfloat16)
    patches = make_patches(normed, CZ)
    reduced = jnp.dot(patches, w_reduce, preferred_element_type=jnp.float32)
    key_input = layer_norm(reduced, gain_keys).astype(jnp.bfloat16)
    tok_cos, tok_sin = token_tables(slab_index * CZ, CZ, HEAD)
    queries = jnp.dot(normed, w_query, preferred_element_type=jnp.float32).reshape(
        tok_rows, heads_dev, HEAD
    )
    queries = rotate(queries, tok_cos, tok_sin).astype(jnp.bfloat16)
    initial = (
        jnp.full((heads_dev, tok_rows), -1e30, jnp.float32),
        jnp.zeros((heads_dev, tok_rows), jnp.float32),
        jnp.zeros((heads_dev, tok_rows, HEAD), jnp.float32),
    )
    state_tuple = initial
    pieces = lax.all_gather(key_input, "slab", axis=0, tiled=True)
    row_count = pieces.shape[0]
    block_rows = math.gcd(row_count, 1024)
    block_count = row_count // block_rows
    blocks = pieces.reshape(block_count, block_rows, pieces.shape[1])

    def one_block(state_inner, block_item):
        rows_in, block_index = block_item
        block_first = block_index * block_rows
        key_cos, key_sin = key_tables(block_first, block_rows, HEAD)
        key_block = jnp.dot(rows_in, w_key, preferred_element_type=jnp.float32).reshape(
            block_rows, heads_dev, HEAD
        )
        key_block = rotate(key_block, key_cos, key_sin).astype(jnp.bfloat16)
        value_block = (
            jnp.dot(rows_in, w_value, preferred_element_type=jnp.float32)
            .astype(jnp.bfloat16)
            .reshape(block_rows, heads_dev, HEAD)
        )
        return (attend_piece(state_inner, queries, key_block, value_block), None)

    state_tuple, _ = lax.scan(
        one_block, state_tuple, (blocks, jnp.arange(block_count, dtype=jnp.int32))
    )
    row_max, row_sum, weighted = state_tuple
    heads_out = (
        (weighted / row_sum[:, :, None])
        .transpose(1, 0, 2)
        .reshape(tok_rows, heads_dev * HEAD)
        .astype(jnp.bfloat16)
    )
    partial_value = jnp.dot(heads_out, w_out, preferred_element_type=jnp.float32)
    head_total = lax.psum(partial_value.astype(jnp.bfloat16), "ffn").astype(jnp.float32)
    attended = head_total.astype(jnp.bfloat16)
    residual = tokens.astype(jnp.float32) + head_total
    normed_ffn = layer_norm(residual, gain_ffn).astype(jnp.bfloat16)
    channels = w_up.shape[1]
    pre = (
        jnp.dot(normed_ffn, w_up, preferred_element_type=jnp.float32)
        .astype(jnp.bfloat16)
        .reshape(CZ, GY, GX, channels)
    )
    pre_wide = padded_2(pre, (("slab", 0),), 1)
    pre_pad = jnp.pad(pre_wide, ((0, 0), (1, 1), (1, 1), (0, 0)))
    mixed = depth_conv(pre_pad, w_depth, CZ).reshape(tok_rows, channels)
    normal_cdf = 0.5 * (1.0 + lax.erf(mixed * ROOT_HALF))
    normal_pdf = jnp.exp(-0.5 * mixed * mixed) * NORMAL_SCALE
    activated = (mixed * normal_cdf).astype(jnp.bfloat16)
    grad_act = jnp.einsum("td,cd->tc", grad_out, w_down, preferred_element_type=jnp.float32)
    grad_mixed = (
        (grad_act * (normal_cdf + mixed * normal_pdf))
        .astype(jnp.bfloat16)
        .reshape(CZ, GY, GX, channels)
    )
    grad_wide = padded_2(grad_mixed, (("slab", 0),), 1)
    grad_pad = jnp.pad(grad_wide, ((0, 0), (1, 1), (1, 1), (0, 0)))
    grad_pre = (
        depth_conv(grad_pad, w_depth[::-1], CZ).astype(jnp.bfloat16).reshape(tok_rows, channels)
    )
    up_full = jnp.einsum("td,tc->dc", normed_ffn, grad_pre, preferred_element_type=jnp.float32)
    down_full = jnp.einsum("td,tc->dc", grad_out, activated, preferred_element_type=jnp.float32)
    grads = lax.psum_scatter(
        jnp.concatenate([up_full, down_full], axis=1), "slab", scatter_dimension=0, tiled=True
    )
    return (attended, grads[:, :channels], grads[:, channels:])


def solution(mesh):
    in_specs = (
        P("slab", None),
        P(),
        P(),
        P(),
        P(None, "ffn"),
        P(None, "ffn"),
        P(None, "ffn"),
        P("ffn", None),
        P(),
        P(None, "ffn"),
        P(None, "ffn"),
        P("ffn", None),
        P("slab", None),
    )
    out_specs = (P("slab", None), P("slab", "ffn"), P("slab", "ffn"))
    return jax.shard_map(
        per_device, mesh=mesh, in_specs=in_specs, out_specs=out_specs, check_vma=False
    )
```

profile of v0, /device:TPU:4, one launch (start us, length us, event | category | flops | bytes accessed | tf_op | source)
XLA Modules:
  0.0 795.7 jit_solution(1866074170113802012)
XLA Ops:
  12.2 3.2 fusion.96
  17.3 306.8 %all-gather.2.cloned.1.call-done = bf16[4096,512]{1,0:T(8,128)(2,1)} async-done(((bf16[64,512]{1,0:T(8,128)(2,1)}), bf16[4096,512]{1,0:T(8,128)(2,1)}) %all-gather.2.cloned.1.call-update) | async-done | bytes 4194320 | tf_op jit(solution)/shard_map/all_gather | solution.py:157
  324.1 48.4 %while.18 = (s32[]{:T(128)}, f32[2,512]{1,0:T(2,128)S(1)}, f32[2,512]{1,0:T(2,128)S(1)}, f32[2,512,64]{1,2,0:T(8,128)S(1)}, bf16[4,1024,512]{2,1,0:T(8,128)(2,1)...) while((s32[]{:T(128)}, f32[2,512]{1,0:T(2,128)S(1)}, ...), condition=%wide.region_7.8_spmd.clone, body=%wide.region_4.7_spmd.clone.sunk | while | flops 546895744 | bytes 35088572 | solution.py:178
  326.0 1.7 fusion.137
  327.8 2.7 bitcast_reduce_fusion.2
  330.5 3.0 fusion.143
  333.6 1.7 convolution_convert_fusion.4
  338.1 1.7 fusion.137
  339.9 2.7 bitcast_reduce_fusion.2
  342.6 3.0 fusion.143
  345.7 1.7 convolution_convert_fusion.4
  350.2 1.7 fusion.137
  352.0 2.7 bitcast_reduce_fusion.2
  354.7 3.0 fusion.143
  357.8 1.7 convolution_convert_fusion.4
  362.3 1.7 fusion.137
  364.1 2.7 bitcast_reduce_fusion.2
  366.9 3.0 fusion.143
  369.9 1.7 convolution_convert_fusion.4
  373.8 41.8 %all-reduce.4.cloned.1.call-done = bf16[512,512]{1,0:T(8,128)(2,1)} async-done(((bf16[512,512]{1,0:T(8,128)(2,1)}), bf16[512,512]{1,0:T(8,128)(2,1)}) %all-reduce.4.cloned.1.call-update) | async-done | bytes 524304 | tf_op jit(solution)/shard_map/psum | solution.py:189
  418.2 1.6 convolution_convert_fusion.1
  419.9 3.7 collective-permute-start
  425.0 10.3 %collective-permute-done = bf16[1,16,16,512]{3,2,1,0:T(8,128)(2,1)S(1)} collective-permute-done((bf16[1,16,16,512]{3,2,1,0:T(8,128)(2,1)S(1)}, bf16[1,16,16,512]{3,2,1,0:T(8,128)(2,1)S(1)}, u32[]{:S(2)}, u32[]{:S(2)}) %collective-permute-start) | collective-permute-done | bytes 262176 | tf_op jit(solution)/shard_map/ppermute | solution.py:25
  435.2 3.5 collective-permute-done.1
  439.5 3.8 multiply_add_fusion
  444.2 1.5 collective-permute-start.2
  445.7 1.5 collective-permute-start.3
  447.7 9.5 %collective-permute-done.2 = bf16[1,16,16,512]{3,2,1,0:T(8,128)(2,1)S(1)} collective-permute-done((bf16[1,16,16,512]{3,2,1,0:T(8,128)(2,1)S(1)}, bf16[1,16,16,512]{3,2,1,0:T(8,128)(2,1)S(1)}, u32[]{:S(2)}, u32[]{:S(2)}) %collective-permute-start.2) | collective-permute-done | bytes 262176 | tf_op jit(solution)/shard_map/ppermute | solution.py:25
  457.2 4.1 collective-permute-done.3
  462.1 3.8 add_convert_fusion.1
  466.8 1.8 copy.31
  468.7 318.3 %reduce-scatter.4.cloned.1.call-done = f32[8,1024]{1,0:T(8,128)} async-done(((f32[512,1024]{1,0:T(8,128)}), f32[8,1024]{1,0:T(8,128)}) %reduce-scatter.4.cloned.1.call-update) | async-done | bytes 32784
  (134 shorter events, 26.5 us)
Async XLA Ops:
  7.2 436.4 %copy-start = (bf16[512,512]{1,0:T(8,128)(2,1)S(1)}, bf16[512,512]{1,0:T(8,128)(2,1)}, u32[]{:S(2)}) copy-start(bf16[512,512]{1,0:T(8,128)(2,1)} %param.27) | copy-start | bytes 1572868
  7.2 316.9 %all-gather.2.cloned.1.call-start = ((), (), s32[]{:S(2)}) async-start(), calls=%async_computation.1 | async-start | bytes 4259840 | tf_op jit(solution)/shard_map/all_gather | solution.py:157
  11.3 4.2 copy-start.11
  11.3 5.1 copy-start.8
  11.7 5.2 copy-start.7
  12.1 311.9 %copy-start.5 = (bf16[512,128]{1,0:T(8,128)(2,1)S(1)}, bf16[512,128]{1,0:T(8,128)(2,1)}, u32[]{:S(2)}) copy-start(bf16[512,128]{1,0:T(8,128)(2,1)} %param.21) | copy-start | bytes 393220
  16.3 399.3 %all-reduce.4.cloned.1.call-start = ((), (), s32[]{:S(2)}) async-start(), calls=%async_computation.2 | async-start | bytes 1048576 | tf_op jit(solution)/shard_map/psum | solution.py:189
  324.1 48.5 %copy-start.9 = (bf16[128,512]{1,0:T(8,128)(2,1)S(1)}, bf16[128,512]{1,0:T(8,128)(2,1)}, u32[]{:S(2)}) copy-start(bf16[128,512]{1,0:T(8,128)(2,1)} %param.22) | copy-start | bytes 393220
  324.1 91.5 %copy-start.2 = (bf16[512,512]{1,0:T(8,128)(2,1)S(1)}, bf16[512,512]{1,0:T(8,128)(2,1)}, u32[]{:S(2)}) copy-start(bf16[512,512]{1,0:T(8,128)(2,1)} %param.15) | copy-start | bytes 1572868
  330.5 4.8 copy-start.1
  342.6 4.8 copy-start.1
  354.7 4.8 copy-start.1
  366.8 4.8 copy-start.1
  372.5 45.7 %copy-start.12 = (bf16[512,512]{1,0:T(8,128)(2,1)S(1)}, bf16[512,512]{1,0:T(8,128)(2,1)}, u32[]{:S(2)}) copy-start(bf16[512,512]{1,0:T(8,128)(2,1)} %param.24) | copy-start | bytes 1572868
  372.5 45.7 %copy-start.13 = (f32[512]{0:T(512)S(1)}, f32[512]{0:T(512)}, u32[]{:S(2)}) copy-start(f32[512]{0:T(512)} %param.23) | copy-start | bytes 6148
  372.6 52.3 %copy-start.10 = (f32[27,512]{1,0:T(8,128)S(1)}, f32[27,512]{1,0:T(8,128)}, u32[]{:S(2)}) copy-start(f32[27,512]{1,0:T(8,128)} %param.25) | copy-start | bytes 165892
  373.8 413.3 %reduce-scatter.4.cloned.1.call-start = ((), (), s32[]{:S(2)}) async-start(), calls=%async_computation.3 | async-start | bytes 2129920
  419.9 15.4 %collective-permute-start = (bf16[1,16,16,512]{3,2,1,0:T(8,128)(2,1)S(1)}, bf16[1,16,16,512]{3,2,1,0:T(8,128)(2,1)S(1)}, u32[]{:S(2)}, u32[]{:S(2)}) collective-permute-start(bf16[1,16,16,512]{3,2,1,0:T(8,128)(2,1)S(1)} %bitcast.133), channel_id=1, source_target_pairs={{0,4},{4,8},{8,12},{12,16},{16,20},{20,24},{24,28},{28,32},{32,36}... | collective-permute-start | bytes 786440 | tf_op jit(solution)/shard_map/ppermute | solution.py:25
  423.6 15.2 %collective-permute-start.1 = (bf16[1,16,16,512]{3,2,1,0:T(8,128)(2,1)S(1)}, bf16[1,16,16,512]{3,2,1,0:T(8,128)(2,1)S(1)}, u32[]{:S(2)}, u32[]{:S(2)}) collective-permute-start(bf16[1,16,16,512]{3,2,1,0:T(8,128)(2,1)S(1)} %bitcast.132), channel_id=1, source_target_pairs={{4,0},{8,4},{12,8},{16,12},{20,16},{24,20},{28,24},{32,28},{36,32}... | collective-permute-start | bytes 786440 | tf_op jit(solution)/shard_map/ppermute | solution.py:27
  439.5 4.1 copy-start.6
  444.2 12.9 %collective-permute-start.2 = (bf16[1,16,16,512]{3,2,1,0:T(8,128)(2,1)S(1)}, bf16[1,16,16,512]{3,2,1,0:T(8,128)(2,1)S(1)}, u32[]{:S(2)}, u32[]{:S(2)}) collective-permute-start(bf16[1,16,16,512]{3,2,1,0:T(8,128)(2,1)S(1)} %bitcast.135), channel_id=1, source_target_pairs={{0,4},{4,8},{8,12},{12,16},{16,20},{20,24},{24,28},{28,32},{32,36}... | collective-permute-start | bytes 786440 | tf_op jit(solution)/shard_map/ppermute | solution.py:25
  445.7 15.6 %collective-permute-start.3 = (bf16[1,16,16,512]{3,2,1,0:T(8,128)(2,1)S(1)}, bf16[1,16,16,512]{3,2,1,0:T(8,128)(2,1)S(1)}, u32[]{:S(2)}, u32[]{:S(2)}) collective-permute-start(bf16[1,16,16,512]{3,2,1,0:T(8,128)(2,1)S(1)} %bitcast.134), channel_id=1, source_target_pairs={{4,0},{8,4},{12,8},{16,12},{20,16},{24,20},{28,24},{32,28},{36,32}... | collective-permute-start | bytes 786440 | tf_op jit(solution)/shard_map/ppermute | solution.py:27
  462.1 3.9 copy-start.3
  466.8 321.6 %copy-start.4 = (bf16[512,512]{1,0:T(8,128)(2,1)S(1)}, bf16[512,512]{1,0:T(8,128)(2,1)}, u32[]{:S(2)}) copy-start(bf16[512,512]{1,0:T(8,128)(2,1)} %all-reduce.4.cloned.1.call-done) | copy-start | bytes 1572868
Sparse Core Ops, SparseCore 0:
  16.4 307.6 all-gather.1
  373.9 41.6 all-reduce.3
  468.8 318.1 reduce-scatter.3
where the time goes:
time: 796 us
  waiting for transfers between devices  694 us (87%)
  matrix products  35.8 us (4%)
  other arithmetic  32.5 us (4%)
  between operations  14.2 us (2%)
  starting transfers between devices  8.07 us (1%)
    unnamed x4, waiting for transfers between devices  318 us
    all_gather x1, waiting for transfers between devices, per_device(): pieces = lax.all_gather(key_input, 'slab', axis=0, tiled=True)  307 us
    psum x1, waiting for transfers between devices, per_device(): lax.psum(partial_value.astype(jnp.bfloat16), 'ffn').astype(jnp.float32)  41.8 us
    ppermute x2, waiting for transfers between devices, padded_2(): lax.ppermute(tail, axis, [(i, (i + 1) % count) for i in range(ends)])  19.8 us
  transfers between devices with their start and end apart: 7, of which 7 were waited for; matrix products, arithmetic and copies ran while one was open for 0% of the time, Pallas kernels for 0%

commit v1 on v0

--- a/solution.py
+++ b/solution.py
@@ -154,7 +154,9 @@
         jnp.zeros((heads_dev, tok_rows, HEAD), jnp.float32),
     )
     state_tuple = initial
-    pieces = lax.all_gather(key_input, "slab", axis=0, tiled=True)
+    pieces = jnp.concatenate(
+        lax.all_to_all(jnp.stack([key_input] * lax.axis_size("slab")), "slab", 0, 0), axis=0
+    )
     row_count = pieces.shape[0]
     block_rows = math.gcd(row_count, 1024)
     block_count = row_count // block_rows

time: 796 us -> 600 us (0.75)
  waiting for transfers between devices: 694 us -> 483 us
  starting transfers between devices: 8.07 us -> 21.2 us
    all_gather x1 -> x0, waiting for transfers between devices: 307 us -> none  [per_device(): pieces = lax.all_gather(key_input, 'slab', axis=0, tiled=True)]
    all_to_all x0 -> x1, waiting for transfers between devices: none -> 95.1 us  [per_device(): lax.all_to_all(jnp.stack([key_input] * lax.axis_size('slab')), 'slab', 0, 0)]
    all_to_all x0 -> x1, starting transfers between devices: none -> 13.1 us  [per_device(): lax.all_to_all(jnp.stack([key_input] * lax.axis_size('slab')), 'slab', 0, 0)]
    unnamed x4 -> x3, waiting for transfers between devices: 318 us -> 319 us
where the time goes in v1:
time: 600 us; the launch traced here: 599 us
  waiting for transfers between devices  483 us (80%)
  matrix products  35.8 us (6%)
  other arithmetic  31.9 us (5%)
  starting transfers between devices  21.2 us (4%)
  between operations  14.5 us (2%)
  local copies, waits for them, and re-layouts  10.1 us (2%)
    unnamed x3, waiting for transfers between devices  319 us
    all_to_all x1, waiting for transfers between devices, per_device(): lax.all_to_all(jnp.stack([key_input] * lax.axis_size('slab')), 'slab', 0, 0)  95.1 us
    psum x1, waiting for transfers between devices, per_device(): lax.psum(partial_value.astype(jnp.bfloat16), 'ffn').astype(jnp.float32)  41.4 us
    ppermute x2, waiting for transfers between devices, padded_2(): lax.ppermute(tail, axis, [(i, (i + 1) % count) for i in range(ends)])  19.8 us
    all_to_all x1, starting transfers between devices, per_device(): lax.all_to_all(jnp.stack([key_input] * lax.axis_size('slab')), 'slab', 0, 0)  13.1 us
    reduce_sum x4, other arithmetic, attend_piece(): row_sum = row_sum * rescale + jnp.sum(expo, axis=2)  12.2 us
  transfers between devices with their start and end apart: 7, of which 7 were waited for; matrix products, arithmetic and copies ran while one was open for 0% of the time, Pallas kernels for 0%

profile of v1, /device:TPU:4, one launch (start us, length us, event | category | flops | bytes accessed | tf_op | source)
XLA Modules:
  0.0 599.1 jit_solution(6627243439894677014)
XLA Ops:
  12.1 3.1 fusion.96
  15.5 2.5 stack.2
  18.0 13.1 %all-to-all-start = ((bf16[64,64,512]{2,1,0:T(8,128)(2,1)}), bf16[64,64,512]{2,1,0:T(8,128)(2,1)}, u32[]{:S(2)}, u32[]{:S(2)}) async-start(bf16[64,64,512]{2,1,0:T(8,128)(2,1)} %stack.2), calls=%async_computation | async-start | bytes 8388608 | tf_op jit(solution)/shard_map/all_to_all | solution.py:158
  32.2 95.1 %all-to-all-done = bf16[64,64,512]{2,1,0:T(8,128)(2,1)} async-done(((bf16[64,64,512]{2,1,0:T(8,128)(2,1)}), bf16[64,64,512]{2,1,0:T(8,128)(2,1)}, u32[]{:S(2)}, u32[]{:S(2)}) %all-to-all-start) | async-done | bytes 4194336 | tf_op jit(solution)/shard_map/all_to_all | solution.py:158
  127.3 48.4 %while.18 = (s32[]{:T(128)}, f32[2,512]{1,0:T(2,128)S(1)}, f32[2,512]{1,0:T(2,128)S(1)}, f32[2,512,64]{1,2,0:T(8,128)S(1)}, bf16[4,1024,512]{2,1,0:T(8,128)(2,1)...) while((s32[]{:T(128)}, f32[2,512]{1,0:T(2,128)S(1)}, ...), condition=%wide.region_7.8_spmd.clone, body=%wide.region_4.7_spmd.clone.sunk | while | flops 546895744 | bytes 35088572 | solution.py:180
  129.2 1.7 fusion.137
  131.0 2.7 bitcast_reduce_fusion.2
  133.7 3.0 fusion.143
  136.8 1.7 convolution_convert_fusion.4
  141.3 1.7 fusion.137
  143.1 2.7 bitcast_reduce_fusion.2
  145.8 3.0 fusion.143
  148.9 1.7 convolution_convert_fusion.4
  153.4 1.7 fusion.137
  155.2 2.7 bitcast_reduce_fusion.2
  157.9 3.0 fusion.143
  161.0 1.7 convolution_convert_fusion.4
  165.5 1.7 fusion.137
  167.3 2.7 bitcast_reduce_fusion.2
  170.1 3.0 fusion.143
  173.1 1.7 convolution_convert_fusion.4
  177.0 41.4 %all-reduce.4.cloned.1.call-done = bf16[512,512]{1,0:T(8,128)(2,1)} async-done(((bf16[512,512]{1,0:T(8,128)(2,1)}), bf16[512,512]{1,0:T(8,128)(2,1)}) %all-reduce.4.cloned.1.call-update) | async-done | bytes 524304 | tf_op jit(solution)/shard_map/psum | solution.py:191
  221.0 1.6 convolution_convert_fusion.1
  222.6 3.7 collective-permute-start
  227.9 10.1 %collective-permute-done = bf16[1,16,16,512]{3,2,1,0:T(8,128)(2,1)S(1)} collective-permute-done((bf16[1,16,16,512]{3,2,1,0:T(8,128)(2,1)S(1)}, bf16[1,16,16,512]{3,2,1,0:T(8,128)(2,1)S(1)}, u32[]{:S(2)}, u32[]{:S(2)}) %collective-permute-start) | collective-permute-done | bytes 262176 | tf_op jit(solution)/shard_map/ppermute | solution.py:25
  238.0 3.5 collective-permute-done.1
  242.3 3.8 multiply_add_fusion
  250.3 9.7 %collective-permute-done.2 = bf16[1,16,16,512]{3,2,1,0:T(8,128)(2,1)S(1)} collective-permute-done((bf16[1,16,16,512]{3,2,1,0:T(8,128)(2,1)S(1)}, bf16[1,16,16,512]{3,2,1,0:T(8,128)(2,1)S(1)}, u32[]{:S(2)}, u32[]{:S(2)}) %collective-permute-start.2) | collective-permute-done | bytes 262176 | tf_op jit(solution)/shard_map/ppermute | solution.py:25
  260.0 4.1 collective-permute-done.3
  264.9 3.8 add_convert_fusion.1
  269.6 1.8 copy.31
  271.4 318.7 %reduce-scatter.4.cloned.1.call-done = f32[8,1024]{1,0:T(8,128)} async-done(((f32[512,1024]{1,0:T(8,128)}), f32[8,1024]{1,0:T(8,128)}) %reduce-scatter.4.cloned.1.call-update) | async-done | bytes 32784
  (134 shorter events, 28.8 us)
Async XLA Ops:
  7.2 239.2 %copy-start = (bf16[512,512]{1,0:T(8,128)(2,1)S(1)}, bf16[512,512]{1,0:T(8,128)(2,1)}, u32[]{:S(2)}) copy-start(bf16[512,512]{1,0:T(8,128)(2,1)} %param.27) | copy-start | bytes 1572868
  11.3 4.2 copy-start.11
  18.0 13.2 %copy-start.8 = (bf16[512,128]{1,0:T(8,128)(2,1)S(1)}, bf16[512,128]{1,0:T(8,128)(2,1)}, u32[]{:S(2)}) copy-start(bf16[512,128]{1,0:T(8,128)(2,1)} %param.20) | copy-start | bytes 393220
  18.0 13.8 %copy-start.7 = (bf16[512,128]{1,0:T(8,128)(2,1)S(1)}, bf16[512,128]{1,0:T(8,128)(2,1)}, u32[]{:S(2)}) copy-start(bf16[512,128]{1,0:T(8,128)(2,1)} %param.19) | copy-start | bytes 393220
  18.0 109.3 %copy-start.5 = (bf16[512,128]{1,0:T(8,128)(2,1)S(1)}, bf16[512,128]{1,0:T(8,128)(2,1)}, u32[]{:S(2)}) copy-start(bf16[512,128]{1,0:T(8,128)(2,1)} %param.21) | copy-start | bytes 393220
  18.0 109.3 %all-to-all-start = ((bf16[64,64,512]{2,1,0:T(8,128)(2,1)}), bf16[64,64,512]{2,1,0:T(8,128)(2,1)}, u32[]{:S(2)}, u32[]{:S(2)}) async-start(bf16[64,64,512]{2,1,0:T(8,128)(2,1)} %stack.2), calls=%async_computation | async-start | bytes 8388608 | tf_op jit(solution)/shard_map/all_to_all | solution.py:158
  31.2 187.2 %all-reduce.4.cloned.1.call-start = ((), (), s32[]{:S(2)}) async-start(), calls=%async_computation.2 | async-start | bytes 1048576 | tf_op jit(solution)/shard_map/psum | solution.py:191
  127.3 48.5 %copy-start.9 = (bf16[128,512]{1,0:T(8,128)(2,1)S(1)}, bf16[128,512]{1,0:T(8,128)(2,1)}, u32[]{:S(2)}) copy-start(bf16[128,512]{1,0:T(8,128)(2,1)} %param.22) | copy-start | bytes 393220
  127.3 91.1 %copy-start.2 = (bf16[512,512]{1,0:T(8,128)(2,1)S(1)}, bf16[512,512]{1,0:T(8,128)(2,1)}, u32[]{:S(2)}) copy-start(bf16[512,512]{1,0:T(8,128)(2,1)} %param.15) | copy-start | bytes 1572868
  133.7 4.8 copy-start.1
  145.8 4.8 copy-start.1
  157.9 4.8 copy-start.1
  170.0 4.8 copy-start.1
  175.7 45.3 %copy-start.12 = (bf16[512,512]{1,0:T(8,128)(2,1)S(1)}, bf16[512,512]{1,0:T(8,128)(2,1)}, u32[]{:S(2)}) copy-start(bf16[512,512]{1,0:T(8,128)(2,1)} %param.24) | copy-start | bytes 1572868
  175.7 45.3 %copy-start.13 = (f32[512]{0:T(512)S(1)}, f32[512]{0:T(512)}, u32[]{:S(2)}) copy-start(f32[512]{0:T(512)} %param.23) | copy-start | bytes 6148
  175.8 52.1 %copy-start.10 = (f32[27,512]{1,0:T(8,128)S(1)}, f32[27,512]{1,0:T(8,128)}, u32[]{:S(2)}) copy-start(f32[27,512]{1,0:T(8,128)} %param.25) | copy-start | bytes 165892
  176.9 413.2 %reduce-scatter.4.cloned.1.call-start = ((), (), s32[]{:S(2)}) async-start(), calls=%async_computation.3 | async-start | bytes 2129920
  222.6 15.4 %collective-permute-start = (bf16[1,16,16,512]{3,2,1,0:T(8,128)(2,1)S(1)}, bf16[1,16,16,512]{3,2,1,0:T(8,128)(2,1)S(1)}, u32[]{:S(2)}, u32[]{:S(2)}) collective-permute-start(bf16[1,16,16,512]{3,2,1,0:T(8,128)(2,1)S(1)} %bitcast.132), channel_id=1, source_target_pairs={{0,4},{4,8},{8,12},{12,16},{16,20},{20,24},{24,28},{28,32},{32,36}... | collective-permute-start | bytes 786440 | tf_op jit(solution)/shard_map/ppermute | solution.py:25
  226.4 15.2 %collective-permute-start.1 = (bf16[1,16,16,512]{3,2,1,0:T(8,128)(2,1)S(1)}, bf16[1,16,16,512]{3,2,1,0:T(8,128)(2,1)S(1)}, u32[]{:S(2)}, u32[]{:S(2)}) collective-permute-start(bf16[1,16,16,512]{3,2,1,0:T(8,128)(2,1)S(1)} %bitcast.131), channel_id=1, source_target_pairs={{4,0},{8,4},{12,8},{16,12},{20,16},{24,20},{28,24},{32,28},{36,32}... | collective-permute-start | bytes 786440 | tf_op jit(solution)/shard_map/ppermute | solution.py:27
  242.3 4.1 copy-start.6
  247.0 12.9 %collective-permute-start.2 = (bf16[1,16,16,512]{3,2,1,0:T(8,128)(2,1)S(1)}, bf16[1,16,16,512]{3,2,1,0:T(8,128)(2,1)S(1)}, u32[]{:S(2)}, u32[]{:S(2)}) collective-permute-start(bf16[1,16,16,512]{3,2,1,0:T(8,128)(2,1)S(1)} %bitcast.134), channel_id=1, source_target_pairs={{0,4},{4,8},{8,12},{12,16},{16,20},{20,24},{24,28},{28,32},{32,36}... | collective-permute-start | bytes 786440 | tf_op jit(solution)/shard_map/ppermute | solution.py:25
  248.5 15.6 %collective-permute-start.3 = (bf16[1,16,16,512]{3,2,1,0:T(8,128)(2,1)S(1)}, bf16[1,16,16,512]{3,2,1,0:T(8,128)(2,1)S(1)}, u32[]{:S(2)}, u32[]{:S(2)}) collective-permute-start(bf16[1,16,16,512]{3,2,1,0:T(8,128)(2,1)S(1)} %bitcast.133), channel_id=1, source_target_pairs={{4,0},{8,4},{12,8},{16,12},{20,16},{24,20},{28,24},{32,28},{36,32}... | collective-permute-start | bytes 786440 | tf_op jit(solution)/shard_map/ppermute | solution.py:27
  264.9 3.9 copy-start.3
  269.6 321.9 %copy-start.4 = (bf16[512,512]{1,0:T(8,128)(2,1)S(1)}, bf16[512,512]{1,0:T(8,128)(2,1)}, u32[]{:S(2)}) copy-start(bf16[512,512]{1,0:T(8,128)(2,1)} %all-reduce.4.cloned.1.call-done) | copy-start | bytes 1572868
Sparse Core Ops, SparseCore 0:
  177.1 41.2 all-reduce.3
  271.6 318.5 reduce-scatter.3
